TPU v7x, 128 devices: a whole 4x4x4 slice. The times are simulated.
128 devices in a mesh: ctx: 16 (over y, z_hi, core), tp: 8 (over z_lo, x).
Axes of the slice: x: 4, y: 4, z: 4 (z_hi: 2, z_lo: 2; z = z_hi * 2 + z_lo), core: 2. Of those that a mesh axis runs over, the one named last changes fastest.
Arguments:
- prompt_states: bfloat16 [2048, 1024], P('ctx'), may hold values from -1.5 to 1.5
- segment_ids: int32 [2048], P('ctx'), may hold values from 0 to 3, never falling along the last dimension, each value on 1 to 1024 neighbouring positions
- past_keys: bfloat16 [2048, 1024], P('ctx', 'tp'), may hold values from -1024 to 1024
- past_values: bfloat16 [2048, 1024], P('ctx', 'tp'), may hold values from -6 to 6
- cache_request: int32 [2048], P('ctx'), may hold values from 0 to 2, as said below
- decode_ids: int32 [4], replicated, may hold values from 0 to 32127
- embed_table: bfloat16 [32128, 1024], P(('ctx', 'tp')), may hold values from -6 to 6
- attn_gain: bfloat16 [1024], replicated, may hold values from 0.25 to 1.75
- ff_gain: bfloat16 [1024], replicated, may hold values from 0.25 to 1.75
- final_gain: bfloat16 [1024], replicated, may hold values from 0.25 to 1.75
- w_query: bfloat16 [1024, 1024], P(None, 'tp'), may hold values from -0.1875 to 0.1875
- w_key: bfloat16 [1024, 1024], P(None, 'tp'), may hold values from -0.1875 to 0.1875
- w_value: bfloat16 [1024, 1024], P(None, 'tp'), may hold values from -0.1875 to 0.1875
- w_out: bfloat16 [1024, 1024], P('tp'), may hold values from -0.1875 to 0.1875
- w_gate: bfloat16 [1024, 2816], P(None, 'tp'), may hold values from -0.1875 to 0.1875
- w_up: bfloat16 [1024, 2816], P(None, 'tp'), may hold values from -0.1875 to 0.1875
- w_down: bfloat16 [2816, 1024], P('tp'), may hold values from -0.109375 to 0.109375
- lm_head: bfloat16 [1024, 32128], P(None, ('ctx', 'tp')), may hold values from -0.1875 to 0.1875
Outputs:
- prompt_out: bfloat16 [2048, 1024], P('ctx')
- logits: float32 [4, 32128], P(None, ('ctx', 'tp'))
- relaid_keys: bfloat16 [2048, 1024], P(('ctx', 'tp'))
- relaid_values: bfloat16 [2048, 1024], P(('ctx', 'tp'))
Inputs may be any that keep to these rules, and one draw needn't show every extreme that they name: `cache_request`: only the even requests have cached rows, which may lie on any devices. `segment_ids`: the tokens of a request are consecutive; a request holds at most 1024 of them, and one request holds exactly that many.
All inputs are finite; a program needn't handle non-finite values.
Results may differ from a plain program's by a relative error of at most 0.03.
Values may be sent and summed in bfloat16 or wider, within the bound.
A program may use at most 64 MiB of HBM per device.

v0:
```python
import jax
import jax.numpy as jnp
from jax import lax
from jax.sharding import PartitionSpec as P

DH = 64
epsilon = 1e-06
scale_factor = 0.125
negative = -1e30


def joined(part, axis, combine):
    gathered = jax.tree.map(lambda a: lax.all_gather(a, axis), part)

    def take(source):
        return jax.tree.map(lambda a: lax.dynamic_index_in_dim(a, source, 0, False), gathered)

    return lax.fori_loop(
        1, lax.axis_size(axis), lambda source, state: combine(state, take(source)), take(0)
    )


def rms_norm(states, gain):
    states = states.astype(jnp.float32)
    mean_square = jnp.mean(states * states, axis=-1, keepdims=True)
    return (states * lax.rsqrt(mean_square + epsilon) * gain.astype(jnp.float32)).astype(
        jnp.bfloat16
    )


def partial_attend(queries, keys, values, allowed):
    scores = (
        jnp.einsum("qhd,khd->qhk", queries, keys, preferred_element_type=jnp.float32) * scale_factor
    )
    scores = jnp.where(allowed[:, None, :], scores, negative)
    highest = jnp.max(scores, axis=2)
    weights = jnp.where(allowed[:, None, :], jnp.exp(scores - highest[:, :, None]), 0.0)
    weight_sum = jnp.sum(weights, axis=2)
    summed = jnp.einsum(
        "qhk,khd->qhd", weights.astype(jnp.bfloat16), values, preferred_element_type=jnp.float32
    )
    return (highest, weight_sum, summed)


def join_parts(earlier, latter):
    highest = jnp.maximum(earlier[0], latter[0])
    left_scale = jnp.exp(earlier[0] - highest)
    right_scale = jnp.exp(latter[0] - highest)
    weight_sum = earlier[1] * left_scale + latter[1] * right_scale
    summed = earlier[2] * left_scale[:, :, None] + latter[2] * right_scale[:, :, None]
    return (highest, weight_sum, summed)


def finish(partials):
    return (partials[2] / partials[1][:, :, None]).astype(jnp.bfloat16)


def fold_block(running, query_heads, block_keys, block_values, allowed):
    key_count = block_keys.shape[0]
    head_group = query_heads.shape[1]

    def attend(current):
        return join_parts(
            current,
            partial_attend(
                query_heads,
                block_keys.reshape(key_count, head_group, DH),
                block_values.reshape(key_count, head_group, DH),
                allowed,
            ),
        )

    def unchanged(current):
        return current

    return lax.cond(jnp.any(allowed), attend, unchanged, running)


def gated_units(normed, w_gate, w_up, w_down):
    gate_value = jnp.dot(normed, w_gate, preferred_element_type=jnp.float32)
    up_value = jnp.dot(normed, w_up, preferred_element_type=jnp.float32)
    hidden = (jax.nn.gelu(gate_value, approximate=True) * up_value).astype(jnp.bfloat16)
    return jnp.dot(hidden, w_down, preferred_element_type=jnp.float32)


def project(normed, weight):
    return jnp.dot(normed, weight, preferred_element_type=jnp.float32).astype(jnp.bfloat16)


def on_device(
    prompt_states,
    segment_ids,
    past_keys,
    past_values,
    cache_request,
    decode_ids,
    embed_table,
    attn_gain,
    ff_gain,
    final_gain,
    w_query,
    w_key,
    w_value,
    w_out,
    w_gate,
    w_up,
    w_down,
    lm_head,
):
    row_count = prompt_states.shape[0]
    head_group = w_query.shape[1] // DH
    ctx_index = lax.axis_index("ctx")
    normed = rms_norm(prompt_states, attn_gain)
    queries = project(normed, w_query)
    keys = project(normed, w_key)
    values = project(normed, w_value)
    query_heads = queries.reshape(row_count, head_group, DH)
    q_positions = ctx_index * row_count + jnp.arange(row_count, dtype=jnp.int32)
    start_parts = (
        jnp.full((row_count, head_group), negative, jnp.float32),
        jnp.zeros((row_count, head_group), jnp.float32),
        jnp.zeros((row_count, head_group, DH), jnp.float32),
    )
    block_keys = lax.all_gather(keys, "ctx", axis=0, tiled=True)
    block_values = lax.all_gather(values, "ctx", axis=0, tiled=True)
    block_segment = lax.all_gather(segment_ids, "ctx", axis=0, tiled=True)
    key_positions = jnp.arange(block_segment.shape[0], dtype=jnp.int32)
    partials = fold_block(
        start_parts,
        query_heads,
        block_keys,
        block_values,
        (segment_ids[:, None] == block_segment[None, :])
        & (key_positions[None, :] <= q_positions[:, None]),
    )
    block_keys = lax.all_gather(past_keys, "ctx", axis=0, tiled=True)
    block_values = lax.all_gather(past_values, "ctx", axis=0, tiled=True)
    block_segment = lax.all_gather(cache_request, "ctx", axis=0, tiled=True)
    partials = fold_block(
        partials,
        query_heads,
        block_keys,
        block_values,
        segment_ids[:, None] == block_segment[None, :],
    )
    attended = finish(partials).reshape(row_count, head_group * DH)
    head_term = jnp.dot(attended, w_out, preferred_element_type=jnp.float32)
    residual = prompt_states.astype(jnp.float32) + lax.psum(
        head_term.astype(jnp.bfloat16), "tp"
    ).astype(jnp.float32)
    unit_term = gated_units(rms_norm(residual, ff_gain), w_gate, w_up, w_down)
    prompt_out = (
        residual + lax.psum(unit_term.astype(jnp.bfloat16), "tp").astype(jnp.float32)
    ).astype(jnp.bfloat16)
    relaid_keys, relaid_values = (
        lax.all_to_all(keys, "tp", split_axis=0, concat_axis=1, tiled=True),
        lax.all_to_all(values, "tp", split_axis=0, concat_axis=1, tiled=True),
    )
    vocab_rows = embed_table.shape[0]
    vocab_start = lax.axis_index(("ctx", "tp")) * vocab_rows
    one_hot = (
        decode_ids[:, None] == vocab_start + jnp.arange(vocab_rows, dtype=jnp.int32)[None, :]
    ).astype(jnp.bfloat16)
    embedded = lax.psum(
        jnp.dot(one_hot, embed_table, preferred_element_type=jnp.float32), ("ctx", "tp")
    )
    request_count = decode_ids.shape[0]
    decode_normed = rms_norm(embedded, attn_gain)
    decode_queries = project(decode_normed, w_query)
    decode_heads = decode_queries.reshape(request_count, head_group, DH)
    decode_keys = project(decode_normed, w_key).reshape(request_count, head_group, DH)
    decode_values = project(decode_normed, w_value).reshape(request_count, head_group, DH)
    requests = jnp.arange(request_count, dtype=jnp.int32)
    cache_count = past_keys.shape[0]
    cache_part = partial_attend(
        decode_heads,
        past_keys.reshape(cache_count, head_group, DH),
        past_values.reshape(cache_count, head_group, DH),
        requests[:, None] == cache_request[None, :],
    )
    prompt_part = partial_attend(
        decode_heads,
        keys.reshape(row_count, head_group, DH),
        values.reshape(row_count, head_group, DH),
        requests[:, None] == segment_ids[None, :],
    )
    gathered = joined(join_parts(prompt_part, cache_part), "ctx", join_parts)
    own_part = partial_attend(
        decode_heads, decode_keys, decode_values, requests[:, None] == requests[None, :]
    )
    decode_attended = finish(join_parts(gathered, own_part)).reshape(request_count, head_group * DH)
    decode_residual = embedded + lax.psum(
        jnp.dot(decode_attended, w_out, preferred_element_type=jnp.float32), "tp"
    )
    decode_term = gated_units(rms_norm(decode_residual, ff_gain), w_gate, w_up, w_down)
    decode_final = decode_residual + lax.psum(decode_term, "tp")
    logits = jnp.dot(
        rms_norm(decode_final, final_gain), lm_head, preferred_element_type=jnp.float32
    )
    return (prompt_out, logits, relaid_keys, relaid_values)


def solution(mesh):
    placed = (
        P("ctx", None),
        P("ctx"),
        P("ctx", "tp"),
        P("ctx", "tp"),
        P("ctx"),
        P(),
        P(("ctx", "tp"), None),
        P(),
        P(),
        P(),
        P(None, "tp"),
        P(None, "tp"),
        P(None, "tp"),
        P("tp", None),
        P(None, "tp"),
        P(None, "tp"),
        P("tp", None),
        P(None, ("ctx", "tp")),
    )
    return jax.shard_map(
        on_device,
        mesh=mesh,
        in_specs=placed,
        out_specs=(
            P("ctx", None),
            P(None, ("ctx", "tp")),
            P(("ctx", "tp"), None),
            P(("ctx", "tp"), None),
        ),
        check_vma=False,
    )
```

profile of v0, /device:TPU:0, one launch (start us, length us, event | category | flops | bytes accessed | tf_op | source)
XLA Modules:
  0.0 462.5 jit_solution(8723615287294162902)
XLA Ops:
  7.3 25.5 %all-gather.2 = s32[16,1,128]{2,1,0:T(1,128)S(1)} all-gather(s32[1,1,128]{2,1,0:T(1,128)} %bitcast.173), channel_id=1, replica_groups=mesh['ctx'=16,'tp'=8] {'ctx'}, dimensions={0}, use_global_device_ids=true | all-gather | bytes 8704 | tf_op jit(solution)/shard_map/all_gather | solution.py:126
  32.8 19.3 %all-gather.1 = s32[16,1,128]{2,1,0:T(1,128)S(1)} all-gather(s32[1,1,128]{2,1,0:T(1,128)} %bitcast.174), channel_id=1, replica_groups=mesh['ctx'=16,'tp'=8] {'ctx'}, dimensions={0}, use_global_device_ids=true | all-gather | bytes 8704 | tf_op jit(solution)/shard_map/all_gather | solution.py:138
  52.1 3.4 fusion.125
  56.8 0.7 convert_element_type.100
  57.4 1.1 fusion.44
  58.5 1.9 convolution_convert_fusion.4
  60.5 23.8 %all_gather.34 = bf16[2048,128]{1,0:T(8,128)(2,1)S(1)} all-gather(bf16[128,128]{1,0:T(8,128)(2,1)} %convolution_convert_fusion.4), channel_id=1, replica_groups=mesh['ctx'=16,'tp'=8] {'ctx'}, dimensions={0}, use_global_device_ids=true | all-gather | bytes 557056 | tf_op jit(solution)/shard_map/all_gather | solution.py:124
  84.3 0.3 convolution_convert_fusion.3
  84.6 0.9 convolution_convert_fusion.2
  85.5 22.3 %all_gather.35 = bf16[2048,128]{1,0:T(8,128)(2,1)} all-gather(bf16[128,128]{1,0:T(8,128)(2,1)} %convolution_convert_fusion.2), channel_id=1, replica_groups=mesh['ctx'=16,'tp'=8] {'ctx'}, dimensions={0}, use_global_device_ids=true | all-gather | bytes 557056 | tf_op jit(solution)/shard_map/all_gather | solution.py:125
  108.0 25.2 %all_gather.36 = bf16[2048,128]{0,1:T(8,128)(2,1)} all-gather(bf16[128,128]{0,1:T(8,128)(2,1)S(1)} %copy.75), channel_id=1, replica_groups=mesh['ctx'=16,'tp'=8] {'ctx'}, dimensions={0}, use_global_device_ids=true | all-gather | bytes 557056 | tf_op jit(solution)/shard_map/all_gather | solution.py:136
  133.3 22.1 %all_gather.37 = bf16[2048,128]{0,1:T(8,128)(2,1)} all-gather(bf16[128,128]{0,1:T(8,128)(2,1)S(1)} %copy.76), channel_id=1, replica_groups=mesh['ctx'=16,'tp'=8] {'ctx'}, dimensions={0}, use_global_device_ids=true | all-gather | bytes 557056 | tf_op jit(solution)/shard_map/all_gather | solution.py:137
  155.4 8.3 %conditional.2 = (f32[128,2]{0,1:T(2,128)}, f32[128,2]{0,1:T(2,128)S(1)}, f32[128,2,64]{0,2,1:T(8,128)S(1)}) conditional(s32[]{:T(128)} %convert_element_type.99, () %tuple.45, (pred[128,2048]{0,1:T(8,128)(4,1)}, bf16[2048,128]{1,0:T(8,128)(2,1)S(1)}, bf16[128,2,64]{0,2,1:T(8,128)(2,1)S(1)}, bf16[2048,128]{1,0:T(8,128)(2,1)}) %tuple.100), branch_computations={%region_3.4_spmd, %region_4.7_spmd} | conditional | flops 138970624 | bytes 11384884 | solution.py:76
  155.4 1.0 copy.73
  156.5 1.8 fusion.131
  158.2 0.6 exponential_multiply_fusion
  158.8 0.4 fusion.3
  159.2 0.7 multiply_add_fusion
  159.9 2.1 copy.74
  162.0 1.7 fusion.5
  163.8 3.6 conditional.3
  163.8 1.8 fusion.132
  165.6 0.4 fusion.14
  166.0 0.7 multiply_add_fusion.1
  166.7 0.7 fusion.16
  167.4 1.0 convolution_convert_fusion.1
  168.4 4.9 %all-to-all-start = ((bf16[8,16,128]{2,1,0:T(8,128)(2,1)}), bf16[8,16,128]{2,1,0:T(8,128)(2,1)S(1)}, u32[]{:S(2)}, u32[]{:S(2)}) async-start(bf16[8,16,128]{2,1,0:T(8,128)(2,1)} %bitcast.34), calls=%async_computation | async-start | bytes 65536 | tf_op jit(solution)/shard_map/all_to_all | solution.py:156
  173.4 0.9 copy.77
  174.3 0.9 copy.81
  175.2 0.2 fusion.70
  175.4 66.9 %psum.37 = f32[4,1024]{1,0:T(4,128)S(1)} all-reduce(f32[4,1024]{1,0:T(4,128)S(1)} %fusion.70), channel_id=1, replica_groups=mesh['ctx'=16,'tp'=8] {'ctx','tp'}, use_global_device_ids=true, to_apply=%region_14.15 | all-reduce | flops 4096 | bytes 32768 | tf_op jit(solution)/shard_map/psum | solution.py:164
  242.5 1.1 convolution_convert_fusion.7
  243.6 1.1 convolution_convert_fusion.6
  244.8 1.2 convolution_convert_fusion.5
  246.0 0.2 fusion.133
  246.2 0.2 fusion.79
  246.4 0.2 fusion.134
  246.6 0.2 fusion.77
  246.8 22.7 %all_gather.38 = f32[16,4,2]{1,2,0:T(2,128)S(1)} all-gather(f32[1,4,2]{1,2,0:T(2,128)S(1)} %get-tuple-element.301), channel_id=1, replica_groups=mesh['ctx'=16,'tp'=8] {'ctx'}, dimensions={0}, use_global_device_ids=true | all-gather | bytes 544 | tf_op jit(solution)/shard_map/all_gather | solution.py:13
  269.5 19.2 %all_gather.39 = f32[16,4,2]{1,2,0:T(2,128)S(1)} all-gather(f32[1,4,2]{1,2,0:T(2,128)S(1)} %get-tuple-element.300), channel_id=1, replica_groups=mesh['ctx'=16,'tp'=8] {'ctx'}, dimensions={0}, use_global_device_ids=true | all-gather | bytes 544 | tf_op jit(solution)/shard_map/all_gather | solution.py:13
  288.7 0.2 fusion.36
  288.9 0.2 fusion.35
  289.1 22.3 %all-gather = f32[64,2,64]{2,1,0:T(2,128)S(1)} all-gather(f32[4,2,64]{2,1,0:T(2,128)S(1)} %copy.83), channel_id=2, replica_groups=mesh['ctx'=16,'tp'=8] {'ctx'}, dimensions={0}, use_global_device_ids=true | all-gather | bytes 34816 | tf_op jit(solution)/shard_map/all_gather | solution.py:13
  311.4 4.4 while.19
  316.0 0.1 fusion.135
  316.1 0.1 fusion.41
  316.3 0.1 reshape.251
  316.4 0.2 fusion.136
  316.6 31.3 %psum.38 = f32[4,1024]{1,0:T(4,128)S(1)} all-reduce(f32[4,1024]{1,0:T(4,128)S(1)} %fusion.136), channel_id=1, replica_groups=mesh['ctx'=16,'tp'=8] {'tp'}, use_global_device_ids=true, to_apply=%region_24.25 | all-reduce | flops 4096 | bytes 32768 | tf_op jit(solution)/shard_map/psum | solution.py:192
  347.9 0.1 multiply_reduce_fusion.2
  348.1 0.3 fusion.119
  348.4 0.7 fusion.42
  349.0 30.6 %psum.39 = f32[4,1024]{1,0:T(4,128)S(1)} all-reduce(f32[4,1024]{1,0:T(4,128)S(1)} %fusion.42), channel_id=1, replica_groups=mesh['ctx'=16,'tp'=8] {'tp'}, use_global_device_ids=true, to_apply=%region_26.27 | all-reduce | flops 4096 | bytes 32768 | tf_op jit(solution)/shard_map/psum | solution.py:196
  379.7 0.1 multiply_reduce_fusion.1
  379.8 0.8 fusion.59
  380.6 1.2 multiply_reduce_fusion
  381.8 1.4 fusion.120
  383.2 1.7 convolution_convert_fusion
  384.9 3.3 all-to-all-start.1
  388.3 0.6 copy_bitcast_fusion.1
  388.9 5.6 %all-to-all-done.1 = bf16[8,16,128]{2,1,0:T(8,128)(2,1)S(1)} async-done(((bf16[8,16,128]{2,1,0:T(8,128)(2,1)}), bf16[8,16,128]{2,1,0:T(8,128)(2,1)S(1)}, u32[]{:S(2)}, u32[]{:S(2)}) %all-to-all-start.1) | async-done | bytes 32800 | tf_op jit(solution)/shard_map/all_to_all | solution.py:157
  394.5 0.6 copy_bitcast_fusion
  395.1 58.8 %all-reduce.5.cloned.1.call-done = bf16[128,1024]{1,0:T(8,128)(2,1)} async-done(((bf16[128,1024]{1,0:T(8,128)(2,1)}), bf16[128,1024]{1,0:T(8,128)(2,1)}) %all-reduce.5.cloned.1.call-update) | async-done | bytes 262160 | tf_op jit(solution)/shard_map/psum | solution.py:153
  453.9 1.8 add_convert_fusion
  (133 shorter events, 5.4 us)
Async XLA Ops:
  7.2 341.2 %copy-start = (bf16[352,1024]{1,0:T(8,128)(2,1)S(1)}, bf16[352,1024]{1,0:T(8,128)(2,1)}, u32[]{:S(2)}) copy-start(bf16[352,1024]{1,0:T(8,128)(2,1)} %param.40) | copy-start | bytes 2162692
  7.2 77.1 %copy-start.1 = (bf16[128,1024]{1,0:T(8,128)(2,1)S(1)}, bf16[128,1024]{1,0:T(8,128)(2,1)}, u32[]{:S(2)}) copy-start(bf16[128,1024]{1,0:T(8,128)(2,1)} %param.24) | copy-start | bytes 786436
  7.2 77.1 %copy-start.10 = (bf16[1024,128]{1,0:T(8,128)(2,1)S(1)}, bf16[1024,128]{1,0:T(8,128)(2,1)}, u32[]{:S(2)}) copy-start(bf16[1024,128]{1,0:T(8,128)(2,1)} %param.34) | copy-start | bytes 786436
  7.2 77.4 %copy-start.11 = (bf16[1024,128]{1,0:T(8,128)(2,1)S(1)}, bf16[1024,128]{1,0:T(8,128)(2,1)}, u32[]{:S(2)}) copy-start(bf16[1024,128]{1,0:T(8,128)(2,1)} %param.36) | copy-start | bytes 786436
  7.2 100.6 %copy-start.12 = (bf16[128,128]{1,0:T(8,128)(2,1)S(1)}, bf16[128,128]{1,0:T(8,128)(2,1)}, u32[]{:S(2)}) copy-start(bf16[128,128]{1,0:T(8,128)(2,1)} %param.26) | copy-start | bytes 98308
  7.2 373.4 %all-reduce.3.cloned.1.call-start = ((), (), s32[]{:S(2)}) async-start(), calls=%async_computation.2 | async-start | bytes 524288 | tf_op jit(solution)/shard_map/psum | solution.py:148
  55.5 77.7 %copy-start.13 = (bf16[128,128]{1,0:T(8,128)(2,1)S(1)}, bf16[128,128]{1,0:T(8,128)(2,1)}, u32[]{:S(2)}) copy-start(bf16[128,128]{1,0:T(8,128)(2,1)} %param.27) | copy-start | bytes 98308
  156.4 2.4 copy-start.5
  163.7 3.7 copy-start.6
  163.7 9.7 %copy-start.18 = (s32[128]{0:T(128)S(1)}, s32[128]{0:T(128)}, u32[]{:S(2)}) copy-start(s32[128]{0:T(128)} %param.28) | copy-start | bytes 1540
  163.7 10.5 %copy-start.16 = (s32[128]{0:T(128)S(1)}, s32[128]{0:T(128)}, u32[]{:S(2)}) copy-start(s32[128]{0:T(128)} %param.25) | copy-start | bytes 1540
  163.7 11.4 %copy-start.7 = (bf16[251,1024]{1,0:T(8,128)(2,1)S(1)}, bf16[251,1024]{1,0:T(8,128)(2,1)}, u32[]{:S(2)}) copy-start(bf16[251,1024]{1,0:T(8,128)(2,1)} %param.30) | copy-start | bytes 1542148
  163.7 11.4 %copy-start.17 = (s32[4]{0:T(128)S(1)}, s32[4]{0:T(128)}, u32[]{:S(2)}) copy-start(s32[4]{0:T(128)} %param.29) | copy-start | bytes 52
  163.8 2.9 copy-start.9
  167.4 78.5 %copy-start.14 = (bf16[1024]{0:T(1024)(128)(2,1)S(1)}, bf16[1024]{0:T(1024)(128)(2,1)}, u32[]{:S(2)}) copy-start(bf16[1024]{0:T(1024)(128)(2,1)} %param.32) | copy-start | bytes 6148
  167.4 180.7 %copy-start.3 = (bf16[1024,352]{0,1:T(8,128)(2,1)S(1)}, bf16[1024,352]{0,1:T(8,128)(2,1)}, u32[]{:S(2)}) copy-start(bf16[1024,352]{0,1:T(8,128)(2,1)} %param.38) | copy-start | bytes 2162692
  168.4 180.0 %copy-start.4 = (bf16[1024,352]{0,1:T(8,128)(2,1)S(1)}, bf16[1024,352]{0,1:T(8,128)(2,1)}, u32[]{:S(2)}) copy-start(bf16[1024,352]{0,1:T(8,128)(2,1)} %param.39) | copy-start | bytes 2162692
  168.4 216.5 %all-to-all-start = ((bf16[8,16,128]{2,1,0:T(8,128)(2,1)}), bf16[8,16,128]{2,1,0:T(8,128)(2,1)S(1)}, u32[]{:S(2)}, u32[]{:S(2)}) async-start(bf16[8,16,128]{2,1,0:T(8,128)(2,1)} %bitcast.34), calls=%async_computation | async-start | bytes 65536 | tf_op jit(solution)/shard_map/all_to_all | solution.py:156
  173.3 280.5 %all-reduce.5.cloned.1.call-start = ((), (), s32[]{:S(2)}) async-start(), calls=%async_computation.3 | async-start | bytes 524288 | tf_op jit(solution)/shard_map/psum | solution.py:153
  244.7 135.1 %copy-start.15 = (bf16[1024]{0:T(1024)(128)(2,1)S(1)}, bf16[1024]{0:T(1024)(128)(2,1)}, u32[]{:S(2)}) copy-start(bf16[1024]{0:T(1024)(128)(2,1)} %param.33) | copy-start | bytes 6148
  244.7 135.1 %copy-start.8 = (bf16[1024,251]{1,0:T(8,128)(2,1)S(1)}, bf16[1024,251]{1,0:T(8,128)(2,1)}, u32[]{:S(2)}) copy-start(bf16[1024,251]{1,0:T(8,128)(2,1)} %param.41) | copy-start | bytes 1542148
  380.6 2.6 copy-start.2
  384.9 9.5 %all-to-all-start.1 = ((bf16[8,16,128]{2,1,0:T(8,128)(2,1)}), bf16[8,16,128]{2,1,0:T(8,128)(2,1)S(1)}, u32[]{:S(2)}, u32[]{:S(2)}) async-start(bf16[8,16,128]{2,1,0:T(8,128)(2,1)} %bitcast.36), calls=%async_computation.1 | async-start | bytes 65536 | tf_op jit(solution)/shard_map/all_to_all | solution.py:157
Sparse Core Ops, SparseCore 0:
  168.5 73.1 all-reduce.2
  385.0 68.7 all-reduce.4
where the time goes:
time: 464 us; the launch traced here: 462 us
  blocking collectives  331 us (71%)
  waiting for transfers between devices  64.4 us (14%)
  matrix products  19.7 us (4%)
  between operations  15.7 us (3%)
  other arithmetic  13.4 us (3%)
  local copies, waits for them, and re-layouts  9.55 us (2%)
  starting transfers between devices  8.32 us (2%)
    psum x1, blocking collectives, on_device(): lax.psum(jnp.dot(one_hot, embed_table, preferred_element_type=jnp.float32...  66.9 us
    all_gather x3, blocking collectives, joined(): gathered = jax.tree.map(lambda a: lax.all_gather(a, axis), part)  64.2 us
    psum x1, waiting for transfers between devices, on_device(): lax.psum(unit_term.astype(jnp.bfloat16), 'tp').astype(jnp.float32)  58.8 us
    psum x1, blocking collectives, on_device(): lax.psum(jnp.dot(decode_attended, w_out, preferred_element_type=jnp.float...  31.3 us
    psum x1, blocking collectives, on_device(): decode_final = decode_residual + lax.psum(decode_term, 'tp')  30.6 us
    all_gather x1, blocking collectives, on_device(): block_segment = lax.all_gather(segment_ids, 'ctx', axis=0, tiled=True)  25.5 us
    all_gather x1, blocking collectives, on_device(): block_keys = lax.all_gather(past_keys, 'ctx', axis=0, tiled=True)  25.2 us
    all_gather x1, blocking collectives, on_device(): block_keys = lax.all_gather(keys, 'ctx', axis=0, tiled=True)  23.8 us
  transfers between devices with their start and end apart: 4, of which 2 were waited for; matrix products, arithmetic and copies ran while one was open for 4% of the time, Pallas kernels for 0%

commit v1 on v0

--- a/solution.py
+++ b/solution.py
@@ -162,7 +162,7 @@
         decode_ids[:, None] == vocab_start + jnp.arange(vocab_rows, dtype=jnp.int32)[None, :]
     ).astype(jnp.bfloat16)
     embedded = lax.psum(
-        jnp.dot(one_hot, embed_table, preferred_element_type=jnp.float32), ("ctx", "tp")
+        lax.psum(jnp.dot(one_hot, embed_table, preferred_element_type=jnp.float32), "tp"), "ctx"
     )
     request_count = decode_ids.shape[0]
     decode_normed = rms_norm(embedded, attn_gain)

time: 464 us -> 494 us (1.065)
  blocking collectives: 331 us -> 360 us
    psum x0 -> x1, blocking collectives: none -> 64.9 us  [on_device(): lax.psum(lax.psum(jnp.dot(one_hot, embed_table, preferred_element_type=jn...]
    psum x1, blocking collectives: 66.9 us -> 34.6 us  [on_device(): lax.psum(jnp.dot(one_hot, embed_table, preferred_element_type=jnp.float32...]
where the time goes in v1:
time: 494 us; the launch traced here: 493 us
  blocking collectives  360 us (73%)
  waiting for transfers between devices  66.2 us (13%)
  matrix products  19.7 us (4%)
  between operations  15.7 us (3%)
  other arithmetic  13.4 us (3%)
  local copies, waits for them, and re-layouts  9.55 us (2%)
  starting transfers between devices  8.32 us (2%)
    psum x1, blocking collectives, on_device(): lax.psum(lax.psum(jnp.dot(one_hot, embed_table, preferred_element_type=jn...  64.9 us
    all_gather x3, blocking collectives, joined(): gathered = jax.tree.map(lambda a: lax.all_gather(a, axis), part)  60.8 us
    psum x1, waiting for transfers between devices, on_device(): lax.psum(unit_term.astype(jnp.bfloat16), 'tp').astype(jnp.float32)  60.6 us
    psum x1, blocking collectives, on_device(): lax.psum(jnp.dot(one_hot, embed_table, preferred_element_type=jnp.float32...  34.6 us
    psum x1, blocking collectives, on_device(): decode_final = decode_residual + lax.psum(decode_term, 'tp')  30.7 us
    psum x1, blocking collectives, on_device(): lax.psum(jnp.dot(decode_attended, w_out, preferred_element_type=jnp.float...  30.6 us
    all_gather x1, blocking collectives, on_device(): block_segment = lax.all_gather(segment_ids, 'ctx', axis=0, tiled=True)  25.5 us
    all_gather x1, blocking collectives, on_device(): block_keys = lax.all_gather(past_keys, 'ctx', axis=0, tiled=True)  25.2 us
  transfers between devices with their start and end apart: 4, of which 2 were waited for; matrix products, arithmetic and copies ran while one was open for 4% of the time, Pallas kernels for 0%

profile of v1, /device:TPU:0, one launch (start us, length us, event | category | flops | bytes accessed | tf_op | source)
XLA Modules:
  0.0 492.8 jit_solution(2330567068291193642)
XLA Ops:
  7.3 25.5 %all-gather.2 = s32[16,1,128]{2,1,0:T(1,128)S(1)} all-gather(s32[1,1,128]{2,1,0:T(1,128)} %bitcast.173), channel_id=1, replica_groups=mesh['ctx'=16,'tp'=8] {'ctx'}, dimensions={0}, use_global_device_ids=true | all-gather | bytes 8704 | tf_op jit(solution)/shard_map/all_gather | solution.py:126
  32.8 19.3 %all-gather.1 = s32[16,1,128]{2,1,0:T(1,128)S(1)} all-gather(s32[1,1,128]{2,1,0:T(1,128)} %bitcast.174), channel_id=1, replica_groups=mesh['ctx'=16,'tp'=8] {'ctx'}, dimensions={0}, use_global_device_ids=true | all-gather | bytes 8704 | tf_op jit(solution)/shard_map/all_gather | solution.py:138
  52.1 3.4 fusion.125
  56.8 0.7 convert_element_type.100
  57.4 1.1 fusion.44
  58.5 1.9 convolution_convert_fusion.4
  60.5 23.8 %all_gather.34 = bf16[2048,128]{1,0:T(8,128)(2,1)S(1)} all-gather(bf16[128,128]{1,0:T(8,128)(2,1)} %convolution_convert_fusion.4), channel_id=1, replica_groups=mesh['ctx'=16,'tp'=8] {'ctx'}, dimensions={0}, use_global_device_ids=true | all-gather | bytes 557056 | tf_op jit(solution)/shard_map/all_gather | solution.py:124
  84.3 0.3 convolution_convert_fusion.3
  84.6 0.9 convolution_convert_fusion.2
  85.5 22.3 %all_gather.35 = bf16[2048,128]{1,0:T(8,128)(2,1)} all-gather(bf16[128,128]{1,0:T(8,128)(2,1)} %convolution_convert_fusion.2), channel_id=1, replica_groups=mesh['ctx'=16,'tp'=8] {'ctx'}, dimensions={0}, use_global_device_ids=true | all-gather | bytes 557056 | tf_op jit(solution)/shard_map/all_gather | solution.py:125
  108.0 25.2 %all_gather.36 = bf16[2048,128]{0,1:T(8,128)(2,1)} all-gather(bf16[128,128]{0,1:T(8,128)(2,1)S(1)} %copy.75), channel_id=1, replica_groups=mesh['ctx'=16,'tp'=8] {'ctx'}, dimensions={0}, use_global_device_ids=true | all-gather | bytes 557056 | tf_op jit(solution)/shard_map/all_gather | solution.py:136
  133.3 22.1 %all_gather.37 = bf16[2048,128]{0,1:T(8,128)(2,1)} all-gather(bf16[128,128]{0,1:T(8,128)(2,1)S(1)} %copy.76), channel_id=1, replica_groups=mesh['ctx'=16,'tp'=8] {'ctx'}, dimensions={0}, use_global_device_ids=true | all-gather | bytes 557056 | tf_op jit(solution)/shard_map/all_gather | solution.py:137
  155.4 8.3 %conditional.2 = (f32[128,2]{0,1:T(2,128)}, f32[128,2]{0,1:T(2,128)S(1)}, f32[128,2,64]{0,2,1:T(8,128)S(1)}) conditional(s32[]{:T(128)} %convert_element_type.99, () %tuple.45, (pred[128,2048]{0,1:T(8,128)(4,1)}, bf16[2048,128]{1,0:T(8,128)(2,1)S(1)}, bf16[128,2,64]{0,2,1:T(8,128)(2,1)S(1)}, bf16[2048,128]{1,0:T(8,128)(2,1)}) %tuple.100), branch_computations={%region_3.4_spmd, %region_4.7_spmd} | conditional | flops 138970624 | bytes 11384884 | solution.py:76
  155.4 1.0 copy.73
  156.5 1.8 fusion.131
  158.2 0.6 exponential_multiply_fusion
  158.8 0.4 fusion.3
  159.2 0.7 multiply_add_fusion
  159.9 2.1 copy.74
  162.0 1.7 fusion.5
  163.8 3.6 conditional.3
  163.8 1.8 fusion.132
  165.6 0.4 fusion.14
  166.0 0.7 multiply_add_fusion.1
  166.7 0.7 fusion.16
  167.4 1.0 convolution_convert_fusion.1
  168.4 4.9 all-to-all-start
  173.4 0.9 copy.77
  174.3 0.9 copy.81
  175.2 0.2 fusion.70
  175.4 34.6 %psum.44 = f32[4,1024]{1,0:T(4,128)S(1)} all-reduce(f32[4,1024]{1,0:T(4,128)S(1)} %fusion.70), channel_id=1, replica_groups=mesh['ctx'=16,'tp'=8] {'tp'}, use_global_device_ids=true, to_apply=%region_14.15 | all-reduce | flops 4096 | bytes 32768 | tf_op jit(solution)/shard_map/psum | solution.py:165
  210.0 64.9 %psum.45 = f32[4,1024]{1,0:T(4,128)S(1)} all-reduce(f32[4,1024]{1,0:T(4,128)S(1)} %psum.44), channel_id=1, replica_groups=mesh['ctx'=16,'tp'=8] {'ctx'}, use_global_device_ids=true, to_apply=%region_15.16 | all-reduce | flops 4096 | bytes 32768 | tf_op jit(solution)/shard_map/psum | solution.py:164
  275.1 1.1 convolution_convert_fusion.7
  276.2 1.1 convolution_convert_fusion.6
  277.4 1.2 convolution_convert_fusion.5
  278.6 0.2 fusion.133
  278.8 0.2 fusion.79
  279.0 0.2 fusion.134
  279.2 0.2 fusion.77
  279.4 19.0 %all_gather.38 = f32[16,4,2]{1,2,0:T(2,128)S(1)} all-gather(f32[1,4,2]{1,2,0:T(2,128)S(1)} %get-tuple-element.301), channel_id=1, replica_groups=mesh['ctx'=16,'tp'=8] {'ctx'}, dimensions={0}, use_global_device_ids=true | all-gather | bytes 544 | tf_op jit(solution)/shard_map/all_gather | solution.py:13
  298.4 22.4 %all_gather.39 = f32[16,4,2]{1,2,0:T(2,128)S(1)} all-gather(f32[1,4,2]{1,2,0:T(2,128)S(1)} %get-tuple-element.300), channel_id=1, replica_groups=mesh['ctx'=16,'tp'=8] {'ctx'}, dimensions={0}, use_global_device_ids=true | all-gather | bytes 544 | tf_op jit(solution)/shard_map/all_gather | solution.py:13
  320.8 0.2 fusion.36
  321.0 0.2 fusion.35
  321.2 19.4 %all-gather = f32[64,2,64]{2,1,0:T(2,128)S(1)} all-gather(f32[4,2,64]{2,1,0:T(2,128)S(1)} %copy.83), channel_id=2, replica_groups=mesh['ctx'=16,'tp'=8] {'ctx'}, dimensions={0}, use_global_device_ids=true | all-gather | bytes 34816 | tf_op jit(solution)/shard_map/all_gather | solution.py:13
  340.6 4.4 while.19
  345.1 0.1 fusion.135
  345.3 0.1 fusion.41
  345.5 0.1 reshape.251
  345.6 0.2 fusion.136
  345.8 30.6 %psum.46 = f32[4,1024]{1,0:T(4,128)S(1)} all-reduce(f32[4,1024]{1,0:T(4,128)S(1)} %fusion.136), channel_id=1, replica_groups=mesh['ctx'=16,'tp'=8] {'tp'}, use_global_device_ids=true, to_apply=%region_25.26 | all-reduce | flops 4096 | bytes 32768 | tf_op jit(solution)/shard_map/psum | solution.py:192
  376.4 0.1 multiply_reduce_fusion.2
  376.5 0.3 fusion.119
  376.8 0.7 fusion.42
  377.5 30.7 %psum.47 = f32[4,1024]{1,0:T(4,128)S(1)} all-reduce(f32[4,1024]{1,0:T(4,128)S(1)} %fusion.42), channel_id=1, replica_groups=mesh['ctx'=16,'tp'=8] {'tp'}, use_global_device_ids=true, to_apply=%region_27.28 | all-reduce | flops 4096 | bytes 32768 | tf_op jit(solution)/shard_map/psum | solution.py:196
  408.3 0.8 fusion.59
  409.1 1.2 multiply_reduce_fusion
  410.3 1.4 fusion.120
  411.7 1.7 convolution_convert_fusion
  413.4 3.3 all-to-all-start.1
  416.8 0.6 copy_bitcast_fusion.1
  417.4 5.6 %all-to-all-done.1 = bf16[8,16,128]{2,1,0:T(8,128)(2,1)S(1)} async-done(((bf16[8,16,128]{2,1,0:T(8,128)(2,1)}), bf16[8,16,128]{2,1,0:T(8,128)(2,1)S(1)}, u32[]{:S(2)}, u32[]{:S(2)}) %all-to-all-start.1) | async-done | bytes 32800 | tf_op jit(solution)/shard_map/all_to_all | solution.py:157
  423.0 0.6 copy_bitcast_fusion
  423.6 60.6 %all-reduce.5.cloned.1.call-done = bf16[128,1024]{1,0:T(8,128)(2,1)} async-done(((bf16[128,1024]{1,0:T(8,128)(2,1)}), bf16[128,1024]{1,0:T(8,128)(2,1)}) %all-reduce.5.cloned.1.call-update) | async-done | bytes 262160 | tf_op jit(solution)/shard_map/psum | solution.py:153
  484.2 1.8 add_convert_fusion
  (134 shorter events, 5.5 us)
Async XLA Ops:
  7.2 369.7 %copy-start = (bf16[352,1024]{1,0:T(8,128)(2,1)S(1)}, bf16[352,1024]{1,0:T(8,128)(2,1)}, u32[]{:S(2)}) copy-start(bf16[352,1024]{1,0:T(8,128)(2,1)} %param.40) | copy-start | bytes 2162692
  7.2 77.1 %copy-start.1 = (bf16[128,1024]{1,0:T(8,128)(2,1)S(1)}, bf16[128,1024]{1,0:T(8,128)(2,1)}, u32[]{:S(2)}) copy-start(bf16[128,1024]{1,0:T(8,128)(2,1)} %param.24) | copy-start | bytes 786436
  7.2 77.1 %copy-start.10 = (bf16[1024,128]{1,0:T(8,128)(2,1)S(1)}, bf16[1024,128]{1,0:T(8,128)(2,1)}, u32[]{:S(2)}) copy-start(bf16[1024,128]{1,0:T(8,128)(2,1)} %param.34) | copy-start | bytes 786436
  7.2 77.4 %copy-start.11 = (bf16[1024,128]{1,0:T(8,128)(2,1)S(1)}, bf16[1024,128]{1,0:T(8,128)(2,1)}, u32[]{:S(2)}) copy-start(bf16[1024,128]{1,0:T(8,128)(2,1)} %param.36) | copy-start | bytes 786436
  7.2 100.6 %copy-start.12 = (bf16[128,128]{1,0:T(8,128)(2,1)S(1)}, bf16[128,128]{1,0:T(8,128)(2,1)}, u32[]{:S(2)}) copy-start(bf16[128,128]{1,0:T(8,128)(2,1)} %param.26) | copy-start | bytes 98308
  7.2 401.9 %all-reduce.3.cloned.1.call-start = ((), (), s32[]{:S(2)}) async-start(), calls=%async_computation.2 | async-start | bytes 524288 | tf_op jit(solution)/shard_map/psum | solution.py:148
  55.5 77.7 %copy-start.13 = (bf16[128,128]{1,0:T(8,128)(2,1)S(1)}, bf16[128,128]{1,0:T(8,128)(2,1)}, u32[]{:S(2)}) copy-start(bf16[128,128]{1,0:T(8,128)(2,1)} %param.27) | copy-start | bytes 98308
  156.4 2.4 copy-start.5
  163.7 3.7 copy-start.6
  163.7 9.7 %copy-start.18 = (s32[128]{0:T(128)S(1)}, s32[128]{0:T(128)}, u32[]{:S(2)}) copy-start(s32[128]{0:T(128)} %param.28) | copy-start | bytes 1540
  163.7 10.5 %copy-start.16 = (s32[128]{0:T(128)S(1)}, s32[128]{0:T(128)}, u32[]{:S(2)}) copy-start(s32[128]{0:T(128)} %param.25) | copy-start | bytes 1540
  163.7 11.4 %copy-start.7 = (bf16[251,1024]{1,0:T(8,128)(2,1)S(1)}, bf16[251,1024]{1,0:T(8,128)(2,1)}, u32[]{:S(2)}) copy-start(bf16[251,1024]{1,0:T(8,128)(2,1)} %param.30) | copy-start | bytes 1542148
  163.7 11.4 %copy-start.17 = (s32[4]{0:T(128)S(1)}, s32[4]{0:T(128)}, u32[]{:S(2)}) copy-start(s32[4]{0:T(128)} %param.29) | copy-start | bytes 52
  163.8 2.9 copy-start.9
  167.4 111.1 %copy-start.14 = (bf16[1024]{0:T(1024)(128)(2,1)S(1)}, bf16[1024]{0:T(1024)(128)(2,1)}, u32[]{:S(2)}) copy-start(bf16[1024]{0:T(1024)(128)(2,1)} %param.32) | copy-start | bytes 6148
  167.4 209.1 %copy-start.3 = (bf16[1024,352]{0,1:T(8,128)(2,1)S(1)}, bf16[1024,352]{0,1:T(8,128)(2,1)}, u32[]{:S(2)}) copy-start(bf16[1024,352]{0,1:T(8,128)(2,1)} %param.38) | copy-start | bytes 2162692
  168.4 208.4 %copy-start.4 = (bf16[1024,352]{0,1:T(8,128)(2,1)S(1)}, bf16[1024,352]{0,1:T(8,128)(2,1)}, u32[]{:S(2)}) copy-start(bf16[1024,352]{0,1:T(8,128)(2,1)} %param.39) | copy-start | bytes 2162692
  168.4 245.0 %all-to-all-start = ((bf16[8,16,128]{2,1,0:T(8,128)(2,1)}), bf16[8,16,128]{2,1,0:T(8,128)(2,1)S(1)}, u32[]{:S(2)}, u32[]{:S(2)}) async-start(bf16[8,16,128]{2,1,0:T(8,128)(2,1)} %bitcast.34), calls=%async_computation | async-start | bytes 65536 | tf_op jit(solution)/shard_map/all_to_all | solution.py:156
  173.3 310.9 %all-reduce.5.cloned.1.call-start = ((), (), s32[]{:S(2)}) async-start(), calls=%async_computation.3 | async-start | bytes 524288 | tf_op jit(solution)/shard_map/psum | solution.py:153
  277.3 131.0 %copy-start.15 = (bf16[1024]{0:T(1024)(128)(2,1)S(1)}, bf16[1024]{0:T(1024)(128)(2,1)}, u32[]{:S(2)}) copy-start(bf16[1024]{0:T(1024)(128)(2,1)} %param.33) | copy-start | bytes 6148
  277.3 131.0 %copy-start.8 = (bf16[1024,251]{1,0:T(8,128)(2,1)S(1)}, bf16[1024,251]{1,0:T(8,128)(2,1)}, u32[]{:S(2)}) copy-start(bf16[1024,251]{1,0:T(8,128)(2,1)} %param.41) | copy-start | bytes 1542148
  409.1 2.6 copy-start.2
  413.4 9.5 %all-to-all-start.1 = ((bf16[8,16,128]{2,1,0:T(8,128)(2,1)}), bf16[8,16,128]{2,1,0:T(8,128)(2,1)S(1)}, u32[]{:S(2)}, u32[]{:S(2)}) async-start(bf16[8,16,128]{2,1,0:T(8,128)(2,1)} %bitcast.36), calls=%async_computation.1 | async-start | bytes 65536 | tf_op jit(solution)/shard_map/all_to_all | solution.py:157
Sparse Core Ops, SparseCore 0:
  168.5 73.0 all-reduce.2
  413.5 70.6 all-reduce.4
